TPU v7x, 32 devices: a whole 2x2x4 slice. The times are simulated.
32 devices in a mesh: dp: 8 (over z, x), mp: 4 (over y, core).
Axes of the slice: x: 2, y: 2, z: 4, core: 2. Of those that a mesh axis runs over, the one named last changes fastest.
Arguments:
- tokens: bfloat16 [256, 48, 3584], P('dp', None, 'mp'), may hold values from -180 to 180
- norm_gain: float32 [3584], replicated, may hold values from 0.1 to 1.9
- w_query: bfloat16 [3584, 3584], P('dp', 'mp'), may hold values from -0.16 to 0.16
- w_keyval: bfloat16 [3584, 2, 512], P('dp', None, 'mp'), may hold values from -0.16 to 0.16
- w_out: bfloat16 [3584, 3584], P('mp', 'dp'), may hold values from -0.09375 to 0.09375
- residents: bfloat16 [8, 2048, 3584], P('dp', 'mp'), may hold values from -6 to 6
- lengths: int32 [256], P('dp'), may hold values from 6 to 48
- cluster: int32 [256, 1], P('dp'), may hold values from 0 to 7; in each aligned block of 32 rows (0 to 31, 32 to 63, ...) at most 4 rows name the same one
- owner: int32 [8], replicated, may hold values from 0 to 7, each once
- counts: int32 [8], replicated, may hold values from 256 to 2048
- flags: int32 [256], P('dp'), may hold values 0 or 1
Outputs:
- similarity: float32 [256, 2048], P('dp', 'mp')
Inputs may be any that keep to these rules, and one draw needn't show every extreme that they name: Each dialogue's cluster; among the 32 dialogues of one index of dp (aligned blocks of rows) no cluster is named more than 4 times. owner gives every cluster a distinct index of dp that holds its residents.
All inputs are finite; a program needn't handle non-finite values. No bound on the sum of `flags` on one device may be relied on, other than what follows from the above.
Results may differ from a plain program's by a relative error of at most 0.013.
Values may be sent and summed in bfloat16 or wider, within the bound.
A program may use at most 128 MiB of HBM per device.

v0:
```python
import math
import jax
import jax.numpy as jnp
from jax import lax
from jax.sharding import PartitionSpec as P

HEAD_DIM = 128
rope_base = 1000000.0
logit_scale = 100.0


def rotate(values, positions):
    half = values.shape[-1] // 2
    freqs = rope_base ** (-jnp.arange(half, dtype=jnp.float32) * 2.0 / values.shape[-1])
    angles = positions.astype(jnp.float32)[:, None] * freqs[None, :]
    cosine = jnp.cos(angles)[:, None, :]
    sine = jnp.sin(angles)[:, None, :]
    first = values[..., :half]
    second = values[..., half:]
    return jnp.concatenate(
        [first * cosine - second * sine, second * cosine + first * sine], axis=-1
    )


def attend(query, keys, values, length):
    seq_len = query.shape[0]
    kv_count = keys.shape[1]
    group = query.shape[1] // kv_count
    grouped = query.reshape(seq_len, kv_count, group, query.shape[-1])
    scores = jnp.einsum(
        "qkgd,pkd->kgqp", grouped, keys, preferred_element_type=jnp.float32
    ) / math.sqrt(query.shape[-1])
    row_pos = jnp.arange(seq_len)[:, None]
    col_pos = jnp.arange(seq_len)[None, :]
    allowed = (col_pos <= row_pos) & (col_pos < length)
    scores = jnp.where(allowed, scores, -1e30)
    highest = jnp.max(scores, axis=-1, keepdims=True)
    expanded = jnp.exp(scores - highest)
    weights = (expanded / jnp.sum(expanded, axis=-1, keepdims=True)).astype(jnp.bfloat16)
    context = jnp.einsum("kgqp,pkd->qkgd", weights, values, preferred_element_type=jnp.float32)
    valid = (jnp.arange(seq_len) < length).astype(jnp.float32)
    pooled = jnp.sum(context * valid[:, None, None, None], axis=0) / length.astype(jnp.float32)
    return pooled.reshape(-1)


def local(
    tokens, norm_gain, w_query, w_keyval, w_out, residents, lengths, cluster, owner, counts, flags
):
    gathered = lax.all_gather(tokens, "mp", axis=2, tiled=True)
    dialogs, seq_len, width = gathered.shape
    hidden = gathered.astype(jnp.float32)
    normed = (
        hidden * lax.rsqrt(jnp.mean(hidden * hidden, axis=-1, keepdims=True) + 1e-06) * norm_gain
    ).astype(jnp.bfloat16)
    normed_flat = normed.reshape(dialogs * seq_len, width)
    query_cols = w_query.shape[1]
    keyval_cols = w_keyval.shape[2]
    pieces = (
        lax.all_gather(w_query, "dp", axis=0, tiled=True),
        lax.all_gather(w_keyval, "dp", axis=0, tiled=True),
    )
    keyval_piece = pieces[1].reshape(pieces[1].shape[0], 2 * keyval_cols)
    query_sum = jnp.dot(normed_flat, pieces[0], preferred_element_type=jnp.float32)
    keyval_sum = jnp.dot(normed_flat, keyval_piece, preferred_element_type=jnp.float32)
    positions = jnp.arange(seq_len)
    local_heads = query_cols // HEAD_DIM
    local_kv = keyval_cols // HEAD_DIM
    query = jax.vmap(lambda block: rotate(block, positions))(
        query_sum.reshape(dialogs, seq_len, local_heads, HEAD_DIM)
    ).astype(jnp.bfloat16)
    keys = jax.vmap(lambda block: rotate(block, positions))(
        keyval_sum[:, :keyval_cols].reshape(dialogs, seq_len, local_kv, HEAD_DIM)
    ).astype(jnp.bfloat16)
    values = (
        keyval_sum[:, keyval_cols:]
        .reshape(dialogs, seq_len, local_kv, HEAD_DIM)
        .astype(jnp.bfloat16)
    )
    pooled_context = jax.vmap(attend)(query, keys, values, lengths).astype(jnp.bfloat16)
    valid = (positions[None, :] < lengths[:, None]).astype(jnp.float32)
    pooled_input = (
        jnp.sum(hidden * valid[:, :, None], axis=1) / lengths.astype(jnp.float32)[:, None]
    )
    partial_out = jnp.dot(
        pooled_context,
        lax.all_gather(w_out, "dp", axis=1, tiled=True),
        preferred_element_type=jnp.float32,
    )
    projected = lax.psum(partial_out.astype(jnp.bfloat16), "mp").astype(jnp.float32)
    embedding = pooled_input + projected
    unit = embedding * lax.rsqrt(jnp.sum(embedding * embedding, axis=-1, keepdims=True) + 1e-06)
    unit = (unit * flags.astype(jnp.float32)[:, None]).astype(jnp.bfloat16)
    my_index = lax.axis_index("dp")
    owner_count = lax.axis_size("dp")
    my_count = jnp.sum(jnp.where(owner == my_index, counts, 0))
    members = residents[0]
    member_count = members.shape[0]
    inverse_norm = lax.rsqrt(
        jnp.einsum("md,md->m", members, members, preferred_element_type=jnp.float32) + 1e-06
    )
    member_start = lax.axis_index("mp") * member_count
    live = member_start + jnp.arange(member_count) < my_count
    table_size = owner.shape[0]
    cluster_ids = cluster[:, 0]
    destination = jnp.sum(
        jnp.where(jnp.arange(table_size)[None, :] == cluster_ids[:, None], owner[None, :], 0),
        axis=1,
    )
    capacity = max(1, -(-dialogs // owner_count))
    order = jnp.arange(dialogs)
    earlier = (destination[None, :] == destination[:, None]) & (order[None, :] < order[:, None])
    rank = jnp.sum(earlier.astype(jnp.int32), axis=1)
    onehot = (jnp.arange(owner_count)[:, None, None] == destination[None, None, :]) & (
        jnp.arange(capacity)[None, :, None] == rank[None, None, :]
    )
    outgoing = jnp.einsum(
        "ocn,nd->ocd", onehot.astype(jnp.bfloat16), unit, preferred_element_type=jnp.float32
    ).astype(jnp.bfloat16)
    query_rows = lax.all_to_all(outgoing, "dp", split_axis=0, concat_axis=0, tiled=True)
    dots = lax.dot_general(
        query_rows,
        members,
        (((query_rows.ndim - 1,), (1,)), ((), ())),
        preferred_element_type=jnp.float32,
    )
    returned = lax.all_to_all(
        jnp.where(live, logit_scale * dots * inverse_norm, 0.0).astype(jnp.bfloat16),
        "dp",
        split_axis=0,
        concat_axis=0,
        tiled=True,
    ).astype(jnp.float32)
    similarity = jnp.einsum(
        "ocn,ocm->nm", onehot.astype(jnp.float32), returned, precision=lax.Precision.HIGHEST
    )
    return similarity


def solution(mesh):
    in_specs = (
        P("dp", None, "mp"),
        P(),
        P("dp", "mp"),
        P("dp", None, "mp"),
        P("mp", "dp"),
        P("dp", "mp", None),
        P("dp"),
        P("dp", None),
        P(),
        P(),
        P("dp"),
    )
    out_specs = P("dp", "mp")
    return jax.shard_map(local, mesh=mesh, in_specs=in_specs, out_specs=out_specs, check_vma=False)
```

profile of v0, /device:TPU:0, one launch (start us, length us, event | category | flops | bytes accessed | tf_op | source)
XLA Modules:
  0.0 408.5 jit_solution(2310838354348667568)
XLA Ops:
  6.5 0.7 all-gather.9.cloned.1.call-update
  7.3 0.0 all-gather.5.cloned.1.call-start
  7.3 0.7 all-gather.5.cloned.1.call-update
  8.0 0.0 all-gather.7.cloned.1.call-start
  8.1 0.7 all-gather.7.cloned.1.call-update
  8.7 0.0 all-gather.11.cloned.1.call-start
  8.8 0.5 all-gather.11.cloned.1.call-update
  9.3 0.0 all-reduce.2.cloned.1.call-start
  9.4 0.7 convert_element_type.91
  10.0 0.7 convert_element_type.99
  10.7 0.8 select_reduce_fusion
  11.5 0.2 convert_reduce_fusion
  11.7 0.7 iota_compare_fusion.1
  12.4 0.2 multiply_cosine_fusion
  12.6 0.3 broadcast_and_fusion
  12.9 2.8 fusion.6
  15.7 97.3 %all-gather.9.cloned.1.call-done = bf16[3584,896]{1,0:T(8,128)(2,1)} async-done(((bf16[448,896]{1,0:T(8,128)(2,1)}), bf16[3584,896]{1,0:T(8,128)(2,1)}) %all-gather.9.cloned.1.call-update) | async-done | bytes 6422544 | tf_op jit(solution)/shard_map/all_gather | solution.py:59
  113.0 9.7 %copy.20 = bf16[896,3584]{1,0:T(8,128)(2,1)} copy(bf16[896,3584]{0,1:T(8,128)(2,1)} %bitcast.86) | data formatting | bytes 12845056 | tf_op jit(solution)/shard_map/dot_general | solution.py:63
  122.7 63.2 %all-gather.5.cloned.1.call-done = bf16[32,48,3584]{2,1,0:T(8,128)(2,1)} async-done(((bf16[32,48,896]{2,1,0:T(8,128)(2,1)}), bf16[32,48,3584]{2,1,0:T(8,128)(2,1)}) %all-gather.5.cloned.1.call-update) | async-done | bytes 11010064 | tf_op jit(solution)/shard_map/all_gather | solution.py:49
  185.8 8.9 %fusion = (f32[32,3584]{1,0:T(8,128)S(1)}, f32[32,48]{1,0:T(8,128)S(1)}) fusion(bf16[32,48,3584]{2,1,0:T(8,128)(2,1)} %all-gather.5.cloned.1.call-done, f32[32,48]{1,0:T(8,128)S(1)} %get-tuple-element.14), kind=kLoop, calls=%fused_computation.3 | loop fusion | flops 27408896 | bytes 11481088 | tf_op jit(solution)/shard_map/reduce_sum | solution.py:82
  194.8 11.0 %fusion.3 = bf16[32,48,3584]{2,1,0:T(8,128)(2,1)} fusion(bf16[32,48,3584]{2,1,0:T(8,128)(2,1)} %all-gather.5.cloned.1.call-done, f32[3584]{0:T(1024)S(1)} %copy-done.1, f32[32,48]{1,0:T(8,128)S(1)} %add_rsqrt_fusion), kind=kLoop, calls=%fused_computation.6 | loop fusion | flops 22020096 | bytes 22040576 | tf_op jit(solution)/shard_map/convert_element_type | solution.py:54
  205.7 28.8 %all-gather.7.cloned.1.call-done = bf16[3584,2,128]{2,1,0:T(2,128)(2,1)} async-done(((bf16[448,2,128]{2,1,0:T(2,128)(2,1)}), bf16[3584,2,128]{2,1,0:T(2,128)(2,1)}) %all-gather.7.cloned.1.call-update) | async-done | bytes 1835024 | tf_op jit(solution)/shard_map/all_gather | solution.py:60
  234.5 7.2 %fusion.22 = f32[1536,256]{1,0:T(8,128)S(1)} fusion(bf16[1536,3584]{1,0:T(8,128)(2,1)} %bitcast.84, bf16[448,8,2,128]{3,2,1,0:T(2,128)(2,1)} %bitcast.92), kind=kOutput, calls=%fused_computation.34 | convolution fusion | flops 2818572288 | bytes 14417920 | tf_op jit(solution)/shard_map/dot_general | solution.py:64
  241.7 0.1 slice.26
  241.8 0.1 slice.48
  241.8 0.3 fusion.36
  242.2 0.2 copy-done
  242.4 1.5 slice-done.1
  243.8 11.6 %fusion.4 = f32[32,48,7,128]{3,1,2,0:T(8,128)S(1)} fusion(bf16[7,128,3584,1]{2,1,0,3:T(8,128)(2,1)S(1)} %bitcast.89, bf16[32,48,3584]{2,1,0:T(8,128)(2,1)S(1)} %copy-done), kind=kOutput, calls=%fused_computation.7 | convolution fusion | flops 9865003008 | bytes 22937600 | tf_op jit(solution)/shard_map/dot_general | solution.py:63
  255.5 1.9 subtract_convert_fusion
  257.4 3.6 fusion.9
  261.0 2.1 fusion.8
  263.2 2.3 fusion.7
  265.5 0.0 copy-start.2
  265.5 0.0 copy-start.3
  265.5 70.8 %all-gather.11.cloned.1.call-done = bf16[896,3584]{0,1:T(8,128)(2,1)} async-done(((bf16[896,448]{0,1:T(8,128)(2,1)}), bf16[896,3584]{0,1:T(8,128)(2,1)}) %all-gather.11.cloned.1.call-update) | async-done | bytes 6422544 | tf_op jit(solution)/shard_map/all_gather | solution.py:86
  336.3 5.5 %convolution_convert_fusion.1 = bf16[32,3584]{1,0:T(8,128)(2,1)} fusion(bf16[896,3584]{0,1:T(8,128)(2,1)} %all-gather.11.cloned.1.call-done, f32[4,8,7,128]{3,2,1,0:T(8,128)S(1)} %bitcast.91, f32[32]{0:T(128)S(1)} %convert_element_type.91), kind=kOutput, calls=%fused_computation.20 | convolution fusion | flops 205692928 | bytes 6766720 | tf_op jit(solution)/shard_map/dot_general | solution.py:84
  341.8 0.0 all-reduce.2.cloned.1.call-update
  341.8 30.2 %all-reduce.2.cloned.1.call-done = bf16[32,3584]{1,0:T(8,128)(2,1)} async-done(((bf16[32,3584]{1,0:T(8,128)(2,1)}), bf16[32,3584]{1,0:T(8,128)(2,1)}) %all-reduce.2.cloned.1.call-update) | async-done | bytes 229392 | tf_op jit(solution)/shard_map/psum | solution.py:89
  372.0 1.2 multiply_reduce_fusion
  373.2 1.9 convolution_convert_fusion
  375.1 5.5 %all-to-all-start = ((bf16[8,4,3584]{2,1,0:T(4,128)(2,1)}), bf16[8,4,3584]{2,1,0:T(4,128)(2,1)S(1)}, u32[]{:S(2)}, u32[]{:S(2)}) async-start(bf16[8,4,3584]{2,1,0:T(4,128)(2,1)} %convolution_convert_fusion), calls=%async_computation | async-start | bytes 458752 | tf_op jit(solution)/shard_map/all_to_all | solution.py:119
  380.7 0.6 fusion.50
  381.3 0.7 add_compare_fusion
  382.0 6.7 %all-to-all-done = bf16[8,4,3584]{2,1,0:T(4,128)(2,1)S(1)} async-done(((bf16[8,4,3584]{2,1,0:T(4,128)(2,1)}), bf16[8,4,3584]{2,1,0:T(4,128)(2,1)S(1)}, u32[]{:S(2)}, u32[]{:S(2)}) %all-to-all-start) | async-done | bytes 229408 | tf_op jit(solution)/shard_map/all_to_all | solution.py:119
  388.7 3.2 fusion.33
  391.9 9.2 %all_to_all.10 = bf16[8,4,512]{2,1,0:T(4,128)(2,1)S(1)} all-to-all(bf16[8,4,512]{2,1,0:T(4,128)(2,1)S(1)} %fusion.33), channel_id=1, replica_groups=mesh['dp'=8,'mp'=4] {'dp'}, dimensions={0} | all-to-all | bytes 65536 | tf_op jit(solution)/shard_map/all_to_all | solution.py:126
  401.2 0.8 convolution_bitcast_fusion
  (19 shorter events, 0.1 us)
Async XLA Ops:
  6.5 106.4 %all-gather.9.cloned.1.call-start = ((), (), s32[]{:S(2)}) async-start(), calls=%async_computation.4 | async-start | bytes 7225344 | tf_op jit(solution)/shard_map/all_gather | solution.py:59
  7.3 178.6 %all-gather.5.cloned.1.call-start = ((), (), s32[]{:S(2)}) async-start(), calls=%async_computation.2 | async-start | bytes 13762560 | tf_op jit(solution)/shard_map/all_gather | solution.py:49
  8.0 226.5 %all-gather.7.cloned.1.call-start = ((), (), s32[]{:S(2)}) async-start(), calls=%async_computation.3 | async-start | bytes 2064384 | tf_op jit(solution)/shard_map/all_gather | solution.py:60
  8.7 327.5 %all-gather.11.cloned.1.call-start = ((), (), s32[]{:S(2)}) async-start(), calls=%async_computation.5 | async-start | bytes 7225344 | tf_op jit(solution)/shard_map/all_gather | solution.py:86
  9.3 362.7 %all-reduce.2.cloned.1.call-start = ((), (), s32[]{:S(2)}) async-start(), calls=%async_computation.6 | async-start | bytes 458752 | tf_op jit(solution)/shard_map/psum | solution.py:89
  185.8 8.9 %copy-start.1 = (f32[3584]{0:T(1024)S(1)}, f32[3584]{0:T(1024)}, u32[]{:S(2)}) copy-start(f32[3584]{0:T(1024)} %param.12) | copy-start | bytes 43012
  194.8 47.4 %slice-start = ((s8[6422528]{0:T(1024)(128)(4,1)}), s8[2228224]{0:T(1024)(128)(4,1)S(1)}, s32[]{:S(2)}) async-start(s8[6422528]{0:T(1024)(128)(4,1)} %bitcast.87), calls=%async_computation.7 | async-start | bytes 4456448
  234.5 7.8 %copy-start = (bf16[32,48,3584]{2,1,0:T(8,128)(2,1)S(1)}, bf16[32,48,3584]{2,1,0:T(8,128)(2,1)}, u32[]{:S(2)}) copy-start(bf16[32,48,3584]{2,1,0:T(8,128)(2,1)} %fusion.3) | copy-start | bytes 33030148
  234.5 9.3 %slice-start.1 = ((s8[6422528]{0:T(1024)(128)(4,1)}), s8[4194304]{0:T(1024)(128)(4,1)S(1)}, s32[]{:S(2)}) async-start(s8[6422528]{0:T(1024)(128)(4,1)} %bitcast.87), calls=%async_computation.8 | async-start | bytes 8388608
  265.5 115.2 %copy-start.2 = (s32[8]{0:T(128)S(1)}, s32[8]{0:T(128)}, u32[]{:S(2)}) copy-start(s32[8]{0:T(128)} %param.19) | copy-start | bytes 100
  265.5 115.2 %copy-start.3 = (s32[8]{0:T(128)S(1)}, s32[8]{0:T(128)}, u32[]{:S(2)}) copy-start(s32[8]{0:T(128)} %param.20) | copy-start | bytes 100
  375.1 13.5 %all-to-all-start = ((bf16[8,4,3584]{2,1,0:T(4,128)(2,1)}), bf16[8,4,3584]{2,1,0:T(4,128)(2,1)S(1)}, u32[]{:S(2)}, u32[]{:S(2)}) async-start(bf16[8,4,3584]{2,1,0:T(4,128)(2,1)} %convolution_convert_fusion), calls=%async_computation | async-start | bytes 458752 | tf_op jit(solution)/shard_map/all_to_all | solution.py:119
Sparse Core Ops, SparseCore 0:
  9.5 103.3 all-gather.8
  114.5 71.2 all-gather.4
  188.0 46.4 all-gather.6
  236.6 99.6 all-gather.10
  341.9 30.0 all-reduce.1
where the time goes:
time: 409 us
  waiting for transfers between devices  299 us (73%)
  matrix products  36.3 us (9%)
  other arithmetic  33 us (8%)
  between operations  13.3 us (3%)
  local copies, waits for them, and re-layouts  11.5 us (3%)
  blocking collectives  9.24 us (2%)
  starting transfers between devices  5.66 us (1%)
    all_gather x1, waiting for transfers between devices, local(): lax.all_gather(w_query, 'dp', axis=0, tiled=True)  97.3 us
    all_gather x1, waiting for transfers between devices, local(): lax.all_gather(w_out, 'dp', axis=1, tiled=True)  70.8 us
    all_gather x1, waiting for transfers between devices, local(): gathered = lax.all_gather(tokens, 'mp', axis=2, tiled=True)  63.2 us
    psum x1, waiting for transfers between devices, local(): lax.psum(partial_out.astype(jnp.bfloat16), 'mp').astype(jnp.float32)  30.2 us
    all_gather x1, waiting for transfers between devices, local(): lax.all_gather(w_keyval, 'dp', axis=0, tiled=True)  28.8 us
    dot_general x1, matrix products, local(): jnp.dot(normed_flat, pieces[0], preferred_element_type=jnp.float32)  11.6 us
    convert_element_type x1, other arithmetic, local(): normed = (hidden * lax.rsqrt(jnp.mean(hidden * hidden, axis=-1, keepdims=...  11 us
    dot_general x1, local copies, waits for them, and re-layouts, local(): jnp.dot(normed_flat, pieces[0], preferred_element_type=jnp.float32)  9.72 us
  transfers between devices with their start and end apart: 6, of which 6 were waited for; matrix products, arithmetic and copies ran while one was open for 16% of the time, Pallas kernels for 0%

commit v1 on v0

--- a/solution.py
+++ b/solution.py
@@ -3,6 +3,7 @@
 import jax.numpy as jnp
 from jax import lax
 from jax.sharding import PartitionSpec as P
+from jax.lax import axis_index, axis_size, ppermute
 
 HEAD_DIM = 128
 rope_base = 1000000.0
@@ -46,7 +47,23 @@
 def local(
     tokens, norm_gain, w_query, w_keyval, w_out, residents, lengths, cluster, owner, counts, flags
 ):
-    gathered = lax.all_gather(tokens, "mp", axis=2, tiled=True)
+
+    def push_page(local_x):
+        num_devices = axis_size("mp")
+        buffer = [local_x]
+        for m in [*range(num_devices - 1)]:
+            buffer.append(
+                ppermute(
+                    buffer[-1],
+                    "mp",
+                    perm=[(tick, (tick + 1) % num_devices) for tick in range(num_devices)],
+                )
+            )
+        return jnp.roll(
+            jnp.concatenate(buffer[::-1], 2), (axis_index("mp") + 1) * local_x.shape[2], 2
+        )
+
+    gathered = push_page(tokens)
     dialogs, seq_len, width = gathered.shape
     hidden = gathered.astype(jnp.float32)
     normed = (

time: 409 us -> 335 us (0.82)
  waiting for transfers between devices: 299 us -> 190 us
  local copies, waits for them, and re-layouts: 11.5 us -> 31.9 us
  other arithmetic: 33 us -> 42.9 us
    all_gather x1, waiting for transfers between devices: 97.3 us -> 0.02 us  [local(): lax.all_gather(w_query, 'dp', axis=0, tiled=True)]
    ppermute x0 -> x3, waiting for transfers between devices: none -> 91.8 us  [push_page(): ppermute(buffer[-1], 'mp', perm=[(tick, (tick + 1) % num_devices) for tic...]
    all_gather x1 -> x0, waiting for transfers between devices: 63.2 us -> none  [local(): gathered = lax.all_gather(tokens, 'mp', axis=2, tiled=True)]
    all_gather x1, waiting for transfers between devices: 28.8 us -> 0.01 us  [local(): lax.all_gather(w_keyval, 'dp', axis=0, tiled=True)]
    unnamed x12 -> x15, local copies, waits for them, and re-layouts: 1.67 us -> 20.3 us
    all_gather x1, waiting for transfers between devices: 70.8 us -> 60 us  [local(): lax.all_gather(w_out, 'dp', axis=1, tiled=True)]
    reduce_sum x1, other arithmetic: 8.89 us -> 17.1 us  [local(): jnp.sum(hidden * valid[:, :, None], axis=1)]
    dot_general x1, matrix products: 11.6 us -> 16.2 us  [local(): jnp.dot(normed_flat, pieces[0], preferred_element_type=jnp.float32)]
  transfers between devices with their start and end apart: 6 -> 8, of which waited for: 6 -> 6; matrix products, arithmetic and copies ran while one was open for 16% -> 31% of each run, Pallas kernels for 0% -> 0%
where the time goes in v1:
time: 335 us; the launch traced here: 334 us
  waiting for transfers between devices  190 us (57%)
  other arithmetic  42.9 us (13%)
  matrix products  40.1 us (12%)
  local copies, waits for them, and re-layouts  31.9 us (10%)
  between operations  13.3 us (4%)
  blocking collectives  9.24 us (3%)
  starting transfers between devices  6.18 us (2%)
    ppermute x3, waiting for transfers between devices, push_page(): ppermute(buffer[-1], 'mp', perm=[(tick, (tick + 1) % num_devices) for tic...  91.8 us
    all_gather x1, waiting for transfers between devices, local(): lax.all_gather(w_out, 'dp', axis=1, tiled=True)  60 us
    psum x1, waiting for transfers between devices, local(): lax.psum(partial_out.astype(jnp.bfloat16), 'mp').astype(jnp.float32)  30.2 us
    unnamed x15, local copies, waits for them, and re-layouts  20.3 us
    reduce_sum x1, other arithmetic, local(): jnp.sum(hidden * valid[:, :, None], axis=1)  17.1 us
    dot_general x1, matrix products, local(): jnp.dot(normed_flat, pieces[0], preferred_element_type=jnp.float32)  16.2 us
    convert_element_type x1, other arithmetic, local(): normed = (hidden * lax.rsqrt(jnp.mean(hidden * hidden, axis=-1, keepdims=...  12.6 us
    dot_general x1, local copies, waits for them, and re-layouts, local(): jnp.dot(normed_flat, pieces[0], preferred_element_type=jnp.float32)  9.71 us
  transfers between devices with their start and end apart: 8, of which 6 were waited for; matrix products, arithmetic and copies ran while one was open for 31% of the time, Pallas kernels for 0%

profile of v1, /device:TPU:0, one launch (start us, length us, event | category | flops | bytes accessed | tf_op | source)
XLA Modules:
  0.0 333.7 jit_solution(12209955997691914518)
XLA Ops:
  6.5 0.7 all-gather.4.cloned.1.call-update
  7.3 0.7 all-gather.6.cloned.1.call-update
  8.1 0.5 collective-permute-start
  8.6 32.9 %collective-permute-done = bf16[32,48,896]{2,1,0:T(8,128)(2,1)S(1)} collective-permute-done((bf16[32,48,896]{2,1,0:T(8,128)(2,1)}, bf16[32,48,896]{2,1,0:T(8,128)(2,1)S(1)}, u32[]{:S(2)}, u32[]{:S(2)}) %collective-permute-start) | collective-permute-done | bytes 2752544 | tf_op jit(solution)/shard_map/ppermute | solution.py:56
  41.5 0.0 collective-permute-start.1
  41.5 32.5 %collective-permute-done.1 = bf16[32,48,896]{2,1,0:T(8,128)(2,1)} collective-permute-done((bf16[32,48,896]{2,1,0:T(8,128)(2,1)S(1)}, bf16[32,48,896]{2,1,0:T(8,128)(2,1)}, u32[]{:S(2)}, u32[]{:S(2)}) %collective-permute-start.1) | collective-permute-done | bytes 2752544 | tf_op jit(solution)/shard_map/ppermute | solution.py:56
  74.1 0.0 all-reduce.2.cloned.1.call-start
  74.2 0.7 convert_element_type.91
  74.8 0.7 convert_element_type.99
  75.5 0.8 select_reduce_fusion
  76.2 0.2 convert_reduce_fusion
  76.5 0.7 iota_compare_fusion.1
  77.2 0.2 multiply_cosine_fusion
  77.4 0.3 broadcast_and_fusion
  77.6 2.9 fusion.6
  80.5 26.4 %collective-permute-done.2 = bf16[32,48,896]{2,1,0:T(8,128)(2,1)} collective-permute-done((bf16[32,48,896]{2,1,0:T(8,128)(2,1)}, bf16[32,48,896]{2,1,0:T(8,128)(2,1)}, u32[]{:S(2)}, u32[]{:S(2)}) %collective-permute-start.2) | collective-permute-done | bytes 2752544 | tf_op jit(solution)/shard_map/ppermute | solution.py:56
  106.8 3.6 %constant_dynamic-update-slice_fusion.7 = bf16[32,48,7168]{2,1,0:T(8,128)(2,1)} fusion(bf16[32,48,896]{2,1,0:T(8,128)(2,1)} %collective-permute-done.2), kind=kLoop, calls=%fused_computation.70 | loop fusion | bytes 5505024
  110.4 3.9 %constant_dynamic-update-slice_fusion.6 = bf16[32,48,7168]{2,1,0:T(8,128)(2,1)} fusion(bf16[32,48,7168]{2,1,0:T(8,128)(2,1)} %constant_dynamic-update-slice_fusion.7, bf16[32,48,896]{2,1,0:T(8,128)(2,1)} %collective-permute-done.1), kind=kLoop, calls=%fused_computation.69 | loop fusion | bytes 5505024
  114.3 1.8 constant_dynamic-update-slice_fusion.5
  116.2 1.9 constant_dynamic-update-slice_fusion.4
  118.0 3.6 %constant_dynamic-update-slice_fusion.3 = bf16[32,48,7168]{2,1,0:T(8,128)(2,1)} fusion(bf16[32,48,7168]{2,1,0:T(8,128)(2,1)} %constant_dynamic-update-slice_fusion.4, bf16[32,48,896]{2,1,0:T(8,128)(2,1)} %collective-permute-done.2), kind=kLoop, calls=%fused_computation.66 | loop fusion | bytes 5505024
  121.7 3.6 %constant_dynamic-update-slice_fusion.2 = bf16[32,48,7168]{2,1,0:T(8,128)(2,1)} fusion(bf16[32,48,7168]{2,1,0:T(8,128)(2,1)} %constant_dynamic-update-slice_fusion.3, bf16[32,48,896]{2,1,0:T(8,128)(2,1)} %collective-permute-done.1), kind=kLoop, calls=%fused_computation.65 | loop fusion | bytes 5505024
  125.3 1.8 constant_dynamic-update-slice_fusion.1
  127.1 1.8 constant_dynamic-update-slice_fusion
  128.9 17.1 %fusion = (f32[32,3584]{1,0:T(8,128)S(1)}, f32[32,48]{1,0:T(8,128)S(1)}) fusion(f32[32,48]{1,0:T(8,128)S(1)} %get-tuple-element.14, bf16[32,48,7168]{2,1,0:T(8,128)(2,1)} %constant_dynamic-update-slice_fusion, s32[]{:T(128)S(6)} %select_n.32), kind=kLoop, calls=%fused_computation.3 | loop fusion | flops 27408896 | bytes 11481092 | tf_op jit(solution)/shard_map/reduce_sum | solution.py:99
  146.0 12.6 %fusion.3 = bf16[32,48,3584]{2,1,0:T(8,128)(2,1)} fusion(f32[3584]{0:T(1024)S(1)} %copy-done.1, f32[32,48]{1,0:T(8,128)S(1)} %add_rsqrt_fusion, bf16[32,48,7168]{2,1,0:T(8,128)(2,1)} %constant_dynamic-update-slice_fusion, s32[]{:T(128)S(6)} %select_n.32), kind=kLoop, calls=%fused_computation.6 | loop fusion | flops 22020096 | bytes 22040580 | tf_op jit(solution)/shard_map/convert_element_type | solution.py:71
  158.6 6.3 %fusion.22 = f32[1536,256]{1,0:T(8,128)S(1)} fusion(bf16[1536,3584]{1,0:T(8,128)(2,1)} %bitcast.84, bf16[448,8,2,128]{3,2,1,0:T(2,128)(2,1)} %bitcast.90), kind=kOutput, calls=%fused_computation.34 | convolution fusion | flops 2818572288 | bytes 14417920 | tf_op jit(solution)/shard_map/dot_general | solution.py:81
  165.0 0.1 slice.26
  165.0 0.1 slice.48
  165.1 0.3 fusion.36
  165.5 9.7 %copy.20 = bf16[896,3584]{1,0:T(8,128)(2,1)} copy(bf16[896,3584]{0,1:T(8,128)(2,1)} %bitcast.86) | data formatting | bytes 12845056 | tf_op jit(solution)/shard_map/dot_general | solution.py:80
  175.2 16.2 %fusion.4 = f32[32,48,7,128]{3,1,2,0:T(8,128)S(1)} fusion(bf16[7,128,3584,1]{2,1,0,3:T(8,128)(2,1)} %bitcast.87, bf16[32,48,3584]{2,1,0:T(8,128)(2,1)} %fusion.3), kind=kOutput, calls=%fused_computation.7 | convolution fusion | flops 9865003008 | bytes 22937600 | tf_op jit(solution)/shard_map/dot_general | solution.py:80
  191.4 1.9 subtract_convert_fusion
  193.4 3.4 %fusion.9 = (f32[32,7,48]{2,1,0:T(8,128)S(1)}, f32[32,48,48,7]{2,1,3,0:T(8,128)S(1)}) fusion(pred[32,48,48]{1,2,0:T(8,128)(4,1)S(1)} %broadcast_and_fusion, bf16[32,48,7,64]{3,1,2,0:T(8,128)(2,1)S(1)} %get-tuple-element.8, bf16[32,48,7,64]{3,1,2,0:T(8,128)(2,1)S(1)} %get-tuple-element.7, bf16[32,48,64]{2,1,0:T(8,128)(2,1)S(1)} %get-tuple-element.10, ...), kind=kOutput, calls=%fused_computation.21 | convolution fusion | flops 139949568 | bytes 5326848 | tf_op jit(solution)/shard_map/vmap(qkgd,pkd->kgqp)/dot_general | solution.py:31
  196.8 2.1 fusion.8
  198.9 2.5 fusion.7
  201.5 60.0 %all-gather.8.cloned.1.call-done = bf16[896,3584]{0,1:T(8,128)(2,1)} async-done(((bf16[896,448]{0,1:T(8,128)(2,1)}), bf16[896,3584]{0,1:T(8,128)(2,1)}) %all-gather.8.cloned.1.call-update) | async-done | bytes 6422544 | tf_op jit(solution)/shard_map/all_gather | solution.py:103
  261.4 5.5 %convolution_convert_fusion.1 = bf16[32,3584]{1,0:T(8,128)(2,1)} fusion(bf16[896,3584]{0,1:T(8,128)(2,1)} %all-gather.8.cloned.1.call-done, f32[4,8,7,128]{3,2,1,0:T(8,128)S(1)} %bitcast.89, f32[32]{0:T(128)S(1)} %convert_element_type.91), kind=kOutput, calls=%fused_computation.20 | convolution fusion | flops 205692928 | bytes 6766720 | tf_op jit(solution)/shard_map/dot_general | solution.py:101
  267.0 30.2 %all-reduce.2.cloned.1.call-done = bf16[32,3584]{1,0:T(8,128)(2,1)} async-done(((bf16[32,3584]{1,0:T(8,128)(2,1)}), bf16[32,3584]{1,0:T(8,128)(2,1)}) %all-reduce.2.cloned.1.call-update) | async-done | bytes 229392 | tf_op jit(solution)/shard_map/psum | solution.py:106
  297.2 1.2 multiply_reduce_fusion
  298.4 1.9 convolution_convert_fusion
  300.3 5.5 %all-to-all-start = ((bf16[8,4,3584]{2,1,0:T(4,128)(2,1)}), bf16[8,4,3584]{2,1,0:T(4,128)(2,1)S(1)}, u32[]{:S(2)}, u32[]{:S(2)}) async-start(bf16[8,4,3584]{2,1,0:T(4,128)(2,1)} %convolution_convert_fusion), calls=%async_computation | async-start | bytes 458752 | tf_op jit(solution)/shard_map/all_to_all | solution.py:136
  305.8 0.6 fusion.50
  306.5 0.7 add_compare_fusion
  307.1 6.7 %all-to-all-done = bf16[8,4,3584]{2,1,0:T(4,128)(2,1)S(1)} async-done(((bf16[8,4,3584]{2,1,0:T(4,128)(2,1)}), bf16[8,4,3584]{2,1,0:T(4,128)(2,1)S(1)}, u32[]{:S(2)}, u32[]{:S(2)}) %all-to-all-start) | async-done | bytes 229408 | tf_op jit(solution)/shard_map/all_to_all | solution.py:136
  313.8 3.2 fusion.33
  317.1 9.2 %all_to_all.10 = bf16[8,4,512]{2,1,0:T(4,128)(2,1)S(1)} all-to-all(bf16[8,4,512]{2,1,0:T(4,128)(2,1)S(1)} %fusion.33), channel_id=1, replica_groups=mesh['dp'=8,'mp'=4] {'dp'}, dimensions={0} | all-to-all | bytes 65536 | tf_op jit(solution)/shard_map/all_to_all | solution.py:143
  326.3 0.8 convolution_bitcast_fusion
  (25 shorter events, 0.2 us)
Async XLA Ops:
  6.5 152.1 %all-gather.4.cloned.1.call-start = ((), (), s32[]{:S(2)}) async-start(), calls=%async_computation.2 | async-start | bytes 2064384 | tf_op jit(solution)/shard_map/all_gather | solution.py:77
  7.3 158.2 %all-gather.6.cloned.1.call-start = ((), (), s32[]{:S(2)}) async-start(), calls=%async_computation.3 | async-start | bytes 7225344 | tf_op jit(solution)/shard_map/all_gather | solution.py:76
  8.0 253.4 %all-gather.8.cloned.1.call-start = ((), (), s32[]{:S(2)}) async-start(), calls=%async_computation.4 | async-start | bytes 7225344 | tf_op jit(solution)/shard_map/all_gather | solution.py:103
  8.1 33.4 %collective-permute-start = (bf16[32,48,896]{2,1,0:T(8,128)(2,1)}, bf16[32,48,896]{2,1,0:T(8,128)(2,1)S(1)}, u32[]{:S(2)}, u32[]{:S(2)}) collective-permute-start(bf16[32,48,896]{2,1,0:T(8,128)(2,1)} %param.11), channel_id=1, source_target_pairs={{0,1},{1,2},{2,3},{3,0},{4,5},{5,6},{6,7},{7,4},{8,9},{9,10},{10,1... | collective-permute-start | bytes 8257544 | tf_op jit(solution)/shard_map/ppermute | solution.py:56
  41.5 32.6 %collective-permute-start.1 = (bf16[32,48,896]{2,1,0:T(8,128)(2,1)S(1)}, bf16[32,48,896]{2,1,0:T(8,128)(2,1)}, u32[]{:S(2)}, u32[]{:S(2)}) collective-permute-start(bf16[32,48,896]{2,1,0:T(8,128)(2,1)S(1)} %collective-permute-done), channel_id=1, source_target_pairs={{0,1},{1,2},{2,3},{3,0},{4,5},{5,6},{6,7},{7,4},{8,9},{9,10},{10,1... | collective-permute-start | bytes 8257544 | tf_op jit(solution)/shard_map/ppermute | solution.py:56
  74.1 32.8 %collective-permute-start.2 = (bf16[32,48,896]{2,1,0:T(8,128)(2,1)}, bf16[32,48,896]{2,1,0:T(8,128)(2,1)}, u32[]{:S(2)}, u32[]{:S(2)}) collective-permute-start(bf16[32,48,896]{2,1,0:T(8,128)(2,1)} %collective-permute-done.1), channel_id=1, source_target_pairs={{0,1},{1,2},{2,3},{3,0},{4,5},{5,6},{6,7},{7,4},{8,9},{9,10},{10,1... | collective-permute-start | bytes 8257544 | tf_op jit(solution)/shard_map/ppermute | solution.py:56
  74.1 223.1 %all-reduce.2.cloned.1.call-start = ((), (), s32[]{:S(2)}) async-start(), calls=%async_computation.5 | async-start | bytes 458752 | tf_op jit(solution)/shard_map/psum | solution.py:106
  110.4 5.7 %copy-start = (bf16[32,48,896]{2,1,0:T(8,128)(2,1)S(1)}, bf16[32,48,896]{2,1,0:T(8,128)(2,1)}, u32[]{:S(2)}) copy-start(bf16[32,48,896]{2,1,0:T(8,128)(2,1)} %param.11) | copy-start | bytes 8257540
  128.9 17.1 %copy-start.1 = (f32[3584]{0:T(1024)S(1)}, f32[3584]{0:T(1024)}, u32[]{:S(2)}) copy-start(f32[3584]{0:T(1024)} %param.12) | copy-start | bytes 43012
  201.4 104.4 %copy-start.2 = (s32[8]{0:T(128)S(1)}, s32[8]{0:T(128)}, u32[]{:S(2)}) copy-start(s32[8]{0:T(128)} %param.19) | copy-start | bytes 100
  201.4 104.4 %copy-start.3 = (s32[8]{0:T(128)S(1)}, s32[8]{0:T(128)}, u32[]{:S(2)}) copy-start(s32[8]{0:T(128)} %param.20) | copy-start | bytes 100
  300.3 13.5 %all-to-all-start = ((bf16[8,4,3584]{2,1,0:T(4,128)(2,1)}), bf16[8,4,3584]{2,1,0:T(4,128)(2,1)S(1)}, u32[]{:S(2)}, u32[]{:S(2)}) async-start(bf16[8,4,3584]{2,1,0:T(4,128)(2,1)} %convolution_convert_fusion), calls=%async_computation | async-start | bytes 458752 | tf_op jit(solution)/shard_map/all_to_all | solution.py:136
Sparse Core Ops, SparseCore 0:
  9.5 48.9 all-gather.3
  60.7 99.6 all-gather.5
  162.6 98.8 all-gather.7
  267.1 30.0 all-reduce.1
